TPU v7x, 128 devices: a whole 4x4x4 slice. The times are simulated.
128 devices in a mesh: gx: 16 (over z, y), gy: 8 (over x, core).
Axes of the slice: x: 4, y: 4, z: 4, core: 2. Of those that a mesh axis runs over, the one named last changes fastest.
Arguments:
- tracers: float32 [8, 16, 4, 36, 64, 128], P('gy', 'gx'), may hold values from -6 to 6
- velocity: float32 [8, 16, 2, 36, 64, 128], P('gy', 'gx'), may hold values from -0.8 to 0.8
- mixing_rate: float32 [8, 16, 35, 64, 128], P('gy', 'gx'), may hold values from 0.05 to 5
- column_depth: float32 [8, 16, 64, 128], P('gy', 'gx'), may hold values from 0.25 to 2.5
- ocean_mask: int32 [8, 28], replicated, may hold values from 0 to 1, as said below
- clinic_list: int32 [8, 16], replicated, may hold values from 0 to 27, as said below
- tropic_list: int32 [8, 32], replicated, may hold values from -1 to 27, as said below
Outputs:
- new_tracers: float32 [8, 16, 4, 36, 64, 128], P('gy', 'gx')
- surface_height: float32 [8, 32, 64, 128], P('gy', 'gx')
Inputs may be any that keep to these rules, and one draw needn't show every extreme that they name: `ocean_mask`: every block row holds exactly 16 ocean blocks. `clinic_list`: row r lists every ocean block column of block row r exactly once. `tropic_list`: row r lists every ocean block column of block row r exactly once and holds -1 elsewhere; the 2 entries of one device are either all -1 or all blocks.
All inputs are finite; a program needn't handle non-finite values.
Results may differ from a plain program's by a relative error of at most 0.0003.
Values sent between devices are 32-bit elements; how exact they have to be, the bound alone decides.
No kernel may reach another device: no remote copies, remote signals or barrier semaphores. Data moves between devices by JAX's collectives and lax.ppermute only.
A program may use at most 128 MiB of HBM per device.

v0:
```python
import jax
import jax.numpy as jnp
from jax import lax
from jax.sharding import PartitionSpec as P

ITERS = 3
diffusion = 0.12
area_term = 0.1
thermal = 0.2
haline = 0.25
cabbeling = 0.05
forcing = 4.0


def passed_along(value, axis, steps):
    count = lax.axis_size(axis)
    leading, last = (max(0, -steps), min(count, count - steps))
    return lax.ppermute(value, axis, [(source, source + steps) for source in range(leading, last)])


def inverse_map(column_list, row_width):
    row_count, slot_count = column_list.shape
    target = jnp.where(column_list < 0, row_width, column_list)
    row_ids = jnp.broadcast_to(
        jnp.arange(row_count, dtype=jnp.int32)[:, None], (row_count, slot_count)
    )
    slot_ids = jnp.broadcast_to(
        jnp.arange(slot_count, dtype=jnp.int32)[None, :], (row_count, slot_count)
    )
    lookup = jnp.zeros((row_count, row_width + 1), jnp.int32).at[row_ids, target].set(slot_ids)
    return lookup[:, :row_width]


def links(columns, row_ids, ocean_mask, inverse):
    row_count, row_width = ocean_mask.shape
    in_use = (columns >= 0).astype(jnp.float32)
    column = jnp.maximum(columns, 0)
    east_col = (column + 1) % row_width
    west_col = (column + row_width - 1) % row_width
    north_row = jnp.minimum(row_ids + 1, row_count - 1)
    south_row = jnp.maximum(row_ids - 1, 0)
    has_north = (row_ids + 1 < row_count).astype(jnp.float32)
    has_south = (row_ids > 0).astype(jnp.float32)
    mask_float = ocean_mask.astype(jnp.float32)
    face_open = (
        in_use * mask_float[row_ids, east_col],
        in_use * mask_float[row_ids, west_col],
        in_use * has_north * mask_float[north_row, column],
        in_use * has_south * mask_float[south_row, column],
    )
    slot_ids = (
        inverse[row_ids, east_col],
        inverse[row_ids, west_col],
        inverse[north_row, column],
        inverse[south_row, column],
    )
    return (face_open, slot_ids)


def divergence(values, speeds, low_side, high_side, low_speed, open_low, open_high, along_axis):
    length = values.shape[along_axis]
    extended = jnp.concatenate(
        [jnp.expand_dims(low_side, along_axis), values, jnp.expand_dims(high_side, along_axis)],
        axis=along_axis,
    )
    face_speed = jnp.concatenate([jnp.expand_dims(low_speed, along_axis), speeds], axis=along_axis)
    behind = lax.slice_in_dim(extended, 0, length + 1, axis=along_axis)
    forward = lax.slice_in_dim(extended, 1, length + 2, axis=along_axis)
    fluxes = face_speed * (0.5 * (behind + forward)) - diffusion * (forward - behind)
    fluxes = jnp.concatenate(
        [
            lax.slice_in_dim(fluxes, 0, 1, axis=along_axis) * open_low,
            lax.slice_in_dim(fluxes, 1, length, axis=along_axis),
            lax.slice_in_dim(fluxes, length, length + 1, axis=along_axis) * open_high,
        ],
        axis=along_axis,
    )
    return lax.slice_in_dim(fluxes, 1, length + 1, axis=along_axis) - lax.slice_in_dim(
        fluxes, 0, length, axis=along_axis
    )


def vertical_mix(stirred, mixing_rate):
    levels = stirred.shape[3]
    coupling = mixing_rate[:, :, None]
    nothing = jnp.zeros_like(coupling[:, :, :, 0])
    interfaces = [coupling[:, :, :, level_index] for level_index in range(levels - 1)]
    above = [nothing] + interfaces
    beneath = interfaces + [nothing]
    factors = []
    partial_sol = []
    for level_index in range(levels):
        diagonal = 1.0 + above[level_index] + beneath[level_index]
        source = stirred[:, :, :, level_index]
        if level_index > 0:
            diagonal = diagonal - above[level_index] * factors[level_index - 1]
            source = source + above[level_index] * partial_sol[level_index - 1]
        factors.append(beneath[level_index] / diagonal)
        partial_sol.append(source / diagonal)
    result_levels = [partial_sol[levels - 1]]
    for level_index in range(levels - 2, -1, -1):
        result_levels.insert(0, partial_sol[level_index] + factors[level_index] * result_levels[0])
    return jnp.stack(result_levels, axis=3)


def tracer_core(tracers, velocity, mixing_rate, halo_values, face_open):
    west_tracer, west_speed, east_tracer, south_tracer, south_speed, north_tracer = halo_values
    open_east, open_west, open_north, open_south = [
        opening[:, :, None, None, None, None] for opening in face_open
    ]
    east_speed = velocity[:, :, 0:1]
    north_speed = velocity[:, :, 1:2]
    stirred = (
        tracers
        - divergence(
            tracers,
            east_speed,
            west_tracer,
            east_tracer,
            west_speed[:, :, None],
            open_west,
            open_east,
            5,
        )
        - divergence(
            tracers,
            north_speed,
            south_tracer,
            north_tracer,
            south_speed[:, :, None],
            open_south,
            open_north,
            4,
        )
    )
    mixed = vertical_mix(stirred, mixing_rate)
    levels = mixed.shape[3]
    spacing = 2.0 * (jnp.arange(levels, dtype=jnp.float32) + 1.0) / (levels * (levels + 1))
    heat = mixed[:, :, 0]
    salinity = mixed[:, :, 1]
    density = haline * salinity - thermal * heat - cabbeling * heat * heat
    column_forcing = forcing * jnp.sum(density * spacing[None, None, :, None, None], axis=2)
    return (mixed, column_forcing)


def face_weights(column_depth, depth_halos, face_open):
    west_depth, east_depth, south_depth, north_depth = depth_halos
    open_east, open_west, open_north, open_south = [
        opening[:, :, None, None] for opening in face_open
    ]
    cells_east = column_depth.shape[3]
    cells_north = column_depth.shape[2]
    edge_east = (jnp.arange(cells_east) == cells_east - 1)[None, None, None, :]
    edge_west = (jnp.arange(cells_east) == 0)[None, None, None, :]
    edge_north = (jnp.arange(cells_north) == cells_north - 1)[None, None, :, None]
    edge_south = (jnp.arange(cells_north) == 0)[None, None, :, None]
    to_east = jnp.concatenate([column_depth[..., 1:], east_depth[..., None]], axis=3)
    to_west = jnp.concatenate([west_depth[..., None], column_depth[..., :-1]], axis=3)
    to_north = jnp.concatenate([column_depth[:, :, 1:], north_depth[:, :, None]], axis=2)
    to_south = jnp.concatenate([south_depth[:, :, None], column_depth[:, :, :-1]], axis=2)
    weight_east = 0.5 * (column_depth + to_east) * jnp.where(edge_east, open_east, 1.0)
    weight_west = 0.5 * (column_depth + to_west) * jnp.where(edge_west, open_west, 1.0)
    weight_north = 0.5 * (column_depth + to_north) * jnp.where(edge_north, open_north, 1.0)
    weight_south = 0.5 * (column_depth + to_south) * jnp.where(edge_south, open_south, 1.0)
    return jnp.stack([weight_east, weight_west, weight_north, weight_south], axis=2)


def apply_operator(values, weights, halo_values):
    east_side, west_side, north_side, south_side = halo_values
    weight_east = weights[:, :, 0]
    weight_west = weights[:, :, 1]
    weight_north = weights[:, :, 2]
    weight_south = weights[:, :, 3]
    to_east = jnp.concatenate([values[..., 1:], east_side[..., None]], axis=3)
    to_west = jnp.concatenate([west_side[..., None], values[..., :-1]], axis=3)
    to_north = jnp.concatenate([values[:, :, 1:], north_side[:, :, None]], axis=2)
    to_south = jnp.concatenate([south_side[:, :, None], values[:, :, :-1]], axis=2)
    return (
        (area_term + weight_east + weight_west + weight_north + weight_south) * values
        - weight_east * to_east
        - weight_west * to_west
        - weight_north * to_north
        - weight_south * to_south
    )


def picked(band_rows, slot_ids):
    return jnp.take(band_rows[0], slot_ids[0], axis=0)[None]


def exchange_edges(values, slot_ids):
    slot_east, slot_west, slot_north, slot_south = slot_ids
    cells_north = values.shape[2]
    side_cols = jnp.concatenate([values[..., -1], values[..., 0]], axis=2)
    from_below = passed_along(values[:, :, -1, :], "gy", 1)
    from_above = passed_along(values[:, :, 0, :], "gy", -1)
    band_sides, band_below, band_above = (
        lax.all_gather(side_cols, "gx", axis=1, tiled=True),
        lax.all_gather(from_below, "gx", axis=1, tiled=True),
        lax.all_gather(from_above, "gx", axis=1, tiled=True),
    )
    return (
        picked(band_sides, slot_east)[..., cells_north:],
        picked(band_sides, slot_west)[..., :cells_north],
        picked(band_above, slot_north),
        picked(band_below, slot_south),
    )


def squares(residual):
    return lax.psum(jnp.sum(residual * residual), ("gx", "gy"))


def solve(forcing_field, weights, slot_ids):
    solution = jnp.zeros_like(forcing_field)
    residual = forcing_field
    direction = forcing_field
    norm_now = squares(residual)
    for iteration in range(ITERS):
        image_field = apply_operator(direction, weights, exchange_edges(direction, slot_ids))
        step_size = norm_now / lax.psum(jnp.sum(direction * image_field), ("gx", "gy"))
        solution = solution + step_size * direction
        if iteration + 1 < ITERS:
            residual = residual - step_size * image_field
            norm_next = squares(residual)
            direction = residual + norm_next / norm_now * direction
            norm_now = norm_next
    return solution


def body(tracers, velocity, mixing_rate, column_depth, ocean_mask, clinic_list, tropic_list):
    band_row = lax.axis_index("gy")
    band_col = lax.axis_index("gx")
    slot_count = tracers.shape[1]
    tracer_count = tracers.shape[2]
    levels = tracers.shape[3]
    cells_north = tracers.shape[4]
    cells_east = tracers.shape[5]
    row_width = ocean_mask.shape[1]
    inverse = inverse_map(clinic_list, row_width)
    clinic_row = lax.dynamic_index_in_dim(clinic_list, band_row, 0, keepdims=False)
    own_columns = lax.dynamic_slice_in_dim(clinic_row, band_col * slot_count, slot_count)[None]
    row_ids = jnp.full((1, slot_count), band_row, jnp.int32)
    face_open, slot_ids = links(own_columns, row_ids, ocean_mask, inverse)
    slot_east, slot_west, slot_north, slot_south = slot_ids
    east_cols = jnp.concatenate(
        [
            tracers[..., -1].reshape(1, slot_count, -1),
            velocity[:, :, 0, :, :, -1].reshape(1, slot_count, -1),
            column_depth[..., -1],
        ],
        axis=2,
    )
    west_cols = jnp.concatenate(
        [tracers[..., 0].reshape(1, slot_count, -1), column_depth[..., 0]], axis=2
    )
    side_cols = jnp.concatenate([east_cols, west_cols], axis=2)
    north_rows = jnp.concatenate(
        [
            tracers[..., -1, :].reshape(1, slot_count, -1),
            velocity[:, :, 1, :, -1, :].reshape(1, slot_count, -1),
            column_depth[..., -1, :],
        ],
        axis=2,
    )
    south_rows = jnp.concatenate(
        [tracers[..., 0, :].reshape(1, slot_count, -1), column_depth[..., 0, :]], axis=2
    )
    band_sides, band_north, band_south = (
        lax.all_gather(side_cols, "gx", axis=1, tiled=True),
        lax.all_gather(north_rows, "gx", axis=1, tiled=True),
        lax.all_gather(south_rows, "gx", axis=1, tiled=True),
    )
    band_below = passed_along(band_north, "gy", 1)
    band_above = passed_along(band_south, "gy", -1)
    tracer_len = tracer_count * levels
    east_len = (tracer_len + levels + 1) * cells_north
    from_west = picked(band_sides, slot_west)[..., :east_len]
    from_east = picked(band_sides, slot_east)[..., east_len:]
    from_south = picked(band_below, slot_south)
    from_north = picked(band_above, slot_north)
    halo_values = (
        from_west[..., : tracer_len * cells_north].reshape(
            1, slot_count, tracer_count, levels, cells_north
        ),
        from_west[..., tracer_len * cells_north : (tracer_len + levels) * cells_north].reshape(
            1, slot_count, levels, cells_north
        ),
        from_east[..., : tracer_len * cells_north].reshape(
            1, slot_count, tracer_count, levels, cells_north
        ),
        from_south[..., : tracer_len * cells_east].reshape(
            1, slot_count, tracer_count, levels, cells_east
        ),
        from_south[..., tracer_len * cells_east : (tracer_len + levels) * cells_east].reshape(
            1, slot_count, levels, cells_east
        ),
        from_north[..., : tracer_len * cells_east].reshape(
            1, slot_count, tracer_count, levels, cells_east
        ),
    )
    depth_halos = (
        from_west[..., (tracer_len + levels) * cells_north :],
        from_east[..., tracer_len * cells_north :],
        from_south[..., (tracer_len + levels) * cells_east :],
        from_north[..., tracer_len * cells_east :],
    )
    new_tracers, column_forcing = tracer_core(
        tracers, velocity, mixing_rate, halo_values, face_open
    )
    weights = face_weights(column_depth, depth_halos, face_open)
    tropic_row = lax.dynamic_index_in_dim(tropic_list, band_row, 0, keepdims=False)
    tropic_count = tropic_list.shape[1] // lax.axis_size("gx")
    own_tropic = lax.dynamic_slice_in_dim(tropic_row, band_col * tropic_count, tropic_count)[None]
    in_use = (own_tropic >= 0)[:, :, None, None]
    inverse_row = lax.dynamic_index_in_dim(inverse, band_row, 0, keepdims=False)
    source_slot = jnp.take(inverse_row, jnp.maximum(own_tropic, 0), axis=0)
    packed = jnp.concatenate([column_forcing[:, :, None], weights], axis=2)
    band_fields = lax.all_gather(packed, "gx", axis=1, tiled=True)
    moved = jnp.where(in_use[..., None], picked(band_fields, source_slot), 0.0)
    tropic_inverse = inverse_map(tropic_list, row_width)
    tropic_ids = jnp.full((1, tropic_count), band_row, jnp.int32)
    tropic_slots = links(own_tropic, tropic_ids, ocean_mask, tropic_inverse)[1]
    surface_height = solve(moved[:, :, 0], moved[:, :, 1:], tropic_slots)
    return (new_tracers, surface_height)


def solution(mesh):
    return jax.shard_map(
        body,
        mesh=mesh,
        in_specs=(
            P("gy", "gx", None, None, None, None),
            P("gy", "gx", None, None, None, None),
            P("gy", "gx", None, None, None),
            P("gy", "gx", None, None),
            P(),
            P(),
            P(),
        ),
        out_specs=(P("gy", "gx", None, None, None, None), P("gy", "gx", None, None)),
        check_vma=False,
    )
```

profile of v0, /device:TPU:1, one launch (start us, length us, event | category | flops | bytes accessed | tf_op | source)
XLA Modules:
  0.0 796.5 jit_solution(15573469216887903358)
XLA Ops:
  7.2 0.7 slice_bitcast_fusion.54
  7.9 1.4 fusion.174
  9.3 0.7 pad_maximum_fusion.4
  10.1 7.6 slice_reduce_fusion
  17.8 0.7 slice_reduce_fusion.2
  18.9 0.9 concatenate.529
  19.9 0.7 pad_maximum_fusion.3
  20.7 5.3 constant_dynamic-update-slice_fusion.1
  30.4 6.4 scatter_fusion
  36.7 5.6 fusion.188
  46.1 1.6 fusion.175
  52.8 1.5 multiply_subtract_fusion.4
  54.3 0.9 slice_bitcast_fusion.37
  55.2 0.9 slice_bitcast_fusion.39
  56.2 5.6 fusion.187
  64.6 3.6 collective-permute-start.1
  68.2 32.6 %all-gather.5.cloned.1.call-done = f32[1,16,20864]{2,0,1:T(1,128)} async-done(((f32[1,1,20864]{2,0,1:T(1,128)}), f32[1,16,20864]{2,0,1:T(1,128)}) %all-gather.5.cloned.1.call-update) | async-done | bytes 1335312 | tf_op jit(solution)/shard_map/all_gather | solution.py:270
  100.8 1.4 copy.184
  102.6 6.8 concatenate.612
  109.5 6.9 concatenate.611
  116.5 1.0 broadcast_in_dim_broadcast_in_dim_reshape.8
  117.5 0.7 fusion.2
  118.2 1.7 copy-done.1
  119.8 3.1 constant_dynamic-update-slice_fusion
  123.0 1.6 copy-done.2
  124.6 5.6 multiply_subtract_fusion
  130.2 3.8 slice.756
  134.0 1.2 copy-done
  135.5 9.8 %slice_multiply_fusion = (f32[1,1,4,36,64,1]{5,4,3,2,1,0:T(8,128)}, f32[1,1,4,36,64,1]{5,4,3,2,1,0:T(8,128)}) fusion(f32[1,1,4,36,64,129]{5,4,3,2,1,0:T(8,128)} %copy-done, f32[]{:T(128)} %bitcast.22, f32[]{:T(128)} %bitcast.21), kind=kLoop, calls=%fused_computation.25 | loop fusion | flops 18432 | bytes 147464 | tf_op jit(solution)/shard_map/mul | solution.py:72
  145.3 1.7 all-gather.7.cloned.1.call-done
  147.0 4.7 collective-permute-start
  151.7 1.0 broadcast_select_fusion.3
  152.7 15.5 %collective-permute-done = f32[1,16,23168]{2,0,1:T(1,128)S(1)} collective-permute-done((f32[1,16,23168]{2,0,1:T(1,128)}, f32[1,16,23168]{2,0,1:T(1,128)S(1)}, u32[]{:S(2)}, u32[]{:S(2)}) %collective-permute-start) | collective-permute-done | bytes 1482784 | tf_op jit(solution)/shard_map/ppermute | solution.py:18
  168.5 4.6 multiply_subtract_fusion.1
  173.2 2.9 slice.762
  176.5 9.6 %fusion.1 = f32[1,1,4,36,64,128]{5,4,3,2,1,0:T(8,128)S(1)} fusion(f32[1,1,4,36,64,128]{5,4,3,2,1,0:T(8,128)S(1)} %bitcast.678, f32[1,1,4,36,64,1]{5,4,3,2,1,0:T(8,128)} %get-tuple-element.253, f32[1,1,4,36,64,127]{5,4,3,2,1,0:T(8,128)S(1)} %bitcast.680, f32[1,1,4,36,64,1]{5,4,3,2,1,0:T(8,128)} %get-tuple-element.252, ...), kind=kLoop, calls=%fused_computation.29 | loop fusion | flops 9437184 | bytes 18984960 | tf_op jit(solution)/shard_map/sub | solution.py:114
  186.4 3.0 add_dynamic-update-slice_fusion
  190.2 2.2 copy-done.8
  193.9 11.2 %scatter_fusion.1 = s32[8,29]{1,0:T(8,128)S(1)} fusion(s32[8,29]{1,0:T(8,128)S(1)} %broadcast.10948.clone.1, s32[256]{0:T(256)S(1)} %reshape.20049, s32[256]{0:T(256)S(1)} %reshape.20051), kind=kCustom, calls=%fused_computation.19 | custom fusion | bytes 5120 | tf_op jit(solution)/shard_map/scatter | solution.py:30
  208.7 31.2 %all-gather.11.cloned.1.call-done = f32[1,16,5,64,128]{4,3,2,0,1:T(8,128)} async-done(((f32[1,1,5,64,128]{4,3,2,0,1:T(8,128)}), f32[1,16,5,64,128]{4,3,2,0,1:T(8,128)}) %all-gather.11.cloned.1.call-update) | async-done | bytes 2621456 | tf_op jit(solution)/shard_map/all_gather | solution.py:319
  239.9 2.3 gather_fusion.1
  242.6 4.0 collective-permute-start.3
  246.6 1.9 collective-permute-start.2
  248.6 17.1 %all_gather.43 = f32[1,32,128]{2,0,1:T(1,128)S(1)} all-gather(f32[1,2,128]{2,0,1:T(1,128)S(1)} %bitcast.718), channel_id=1, replica_groups=mesh['gx'=16,'gy'=8] {'gx'}, dimensions={1}, use_global_device_ids=true | all-gather | bytes 17408 | tf_op jit(solution)/shard_map/all_gather | solution.py:198
  267.3 16.0 %all_gather.45 = f32[1,32,128]{2,0,1:T(1,128)S(1)} all-gather(f32[1,2,128]{2,0,1:T(1,128)S(1)} %bitcast.724), channel_id=1, replica_groups=mesh['gx'=16,'gy'=8] {'gx'}, dimensions={1}, use_global_device_ids=true | all-gather | bytes 17408 | tf_op jit(solution)/shard_map/all_gather | solution.py:199
  283.3 17.3 %all_gather.44 = f32[1,32,128]{2,0,1:T(1,128)S(1)} all-gather(f32[1,2,128]{2,0,1:T(1,128)S(1)} %bitcast.723), channel_id=1, replica_groups=mesh['gx'=16,'gy'=8] {'gx'}, dimensions={1}, use_global_device_ids=true | all-gather | bytes 17408 | tf_op jit(solution)/shard_map/all_gather | solution.py:200
  301.8 0.7 multiply_reduce_fusion.3
  302.5 78.7 %all-reduce.4 = (f32[]{:T(128)}, f32[]{:T(128)}) all-reduce(f32[]{:T(128)} %get-tuple-element.130, f32[]{:T(128)} %get-tuple-element.129), channel_id=1, replica_groups=mesh['gx'=16,'gy'=8] {'gx','gy'}, use_global_device_ids=true, to_apply=%region_3.5 | all-reduce | flops 2 | bytes 16 | tf_op jit(solution)/shard_map/psum | solution.py:211
  383.1 64.1 %psum.44 = f32[]{:T(128)} all-reduce(f32[]{:T(128)} %get-tuple-element.143), channel_id=1, replica_groups=mesh['gx'=16,'gy'=8] {'gx','gy'}, use_global_device_ids=true, to_apply=%region_8.11 | all-reduce | flops 1 | bytes 8 | tf_op jit(solution)/shard_map/psum | solution.py:211
  448.8 15.5 %all_gather.46 = f32[1,32,128]{2,0,1:T(1,128)S(1)} all-gather(f32[1,2,128]{2,0,1:T(1,128)S(1)} %bitcast.719), channel_id=1, replica_groups=mesh['gx'=16,'gy'=8] {'gx'}, dimensions={1}, use_global_device_ids=true | all-gather | bytes 17408 | tf_op jit(solution)/shard_map/all_gather | solution.py:198
  465.5 9.1 %collective-permute-start.5 = (f32[1,2,128]{2,1,0:T(2,128)S(1)}, f32[1,2,128]{2,1,0:T(2,128)S(1)}, u32[]{:S(2)}, u32[]{:S(2)}) collective-permute-start(f32[1,2,128]{2,1,0:T(2,128)S(1)} %bitcast.733), channel_id=1, source_target_pairs={{0,1},{1,2},{2,3},{3,4},{4,5},{5,6},{6,7},{8,9},{9,10},{10,11},{11... | collective-permute-start | bytes 3080 | tf_op jit(solution)/shard_map/ppermute | solution.py:18
  474.6 1.9 collective-permute-start.4
  477.0 16.0 %all_gather.48 = f32[1,32,128]{2,0,1:T(1,128)S(1)} all-gather(f32[1,2,128]{2,0,1:T(1,128)S(1)} %bitcast.726), channel_id=1, replica_groups=mesh['gx'=16,'gy'=8] {'gx'}, dimensions={1}, use_global_device_ids=true | all-gather | bytes 17408 | tf_op jit(solution)/shard_map/all_gather | solution.py:199
  493.6 17.0 %all_gather.47 = f32[1,32,128]{2,0,1:T(1,128)S(1)} all-gather(f32[1,2,128]{2,0,1:T(1,128)S(1)} %bitcast.725), channel_id=1, replica_groups=mesh['gx'=16,'gy'=8] {'gx'}, dimensions={1}, use_global_device_ids=true | all-gather | bytes 17408 | tf_op jit(solution)/shard_map/all_gather | solution.py:200
  511.2 0.7 multiply_reduce_fusion.1
  511.9 73.0 %psum.45 = f32[]{:T(128)} all-reduce(f32[]{:T(128)} %get-tuple-element.141), channel_id=1, replica_groups=mesh['gx'=16,'gy'=8] {'gx','gy'}, use_global_device_ids=true, to_apply=%region_10.13 | all-reduce | flops 1 | bytes 8 | tf_op jit(solution)/shard_map/psum | solution.py:221
  586.9 64.5 %psum.46 = f32[]{:T(128)} all-reduce(f32[]{:T(128)} %multiply_reduce_fusion), channel_id=1, replica_groups=mesh['gx'=16,'gy'=8] {'gx','gy'}, use_global_device_ids=true, to_apply=%region_12.15 | all-reduce | flops 1 | bytes 8 | tf_op jit(solution)/shard_map/psum | solution.py:211
  653.0 15.6 %all_gather.49 = f32[1,32,128]{2,0,1:T(1,128)S(1)} all-gather(f32[1,2,128]{2,0,1:T(1,128)S(1)} %bitcast.720), channel_id=1, replica_groups=mesh['gx'=16,'gy'=8] {'gx'}, dimensions={1}, use_global_device_ids=true | all-gather | bytes 17408 | tf_op jit(solution)/shard_map/all_gather | solution.py:198
  670.1 7.8 collective-permute-start.6
  678.1 3.4 collective-permute-start.7
  681.5 16.4 %all_gather.50 = f32[1,32,128]{2,0,1:T(1,128)S(1)} all-gather(f32[1,2,128]{2,0,1:T(1,128)S(1)} %bitcast.728), channel_id=1, replica_groups=mesh['gx'=16,'gy'=8] {'gx'}, dimensions={1}, use_global_device_ids=true | all-gather | bytes 17408 | tf_op jit(solution)/shard_map/all_gather | solution.py:200
  698.5 16.3 %all_gather.51 = f32[1,32,128]{2,0,1:T(1,128)S(1)} all-gather(f32[1,2,128]{2,0,1:T(1,128)S(1)} %bitcast.727), channel_id=1, replica_groups=mesh['gx'=16,'gy'=8] {'gx'}, dimensions={1}, use_global_device_ids=true | all-gather | bytes 17408 | tf_op jit(solution)/shard_map/all_gather | solution.py:199
  715.4 0.7 fusion.60
  716.1 71.9 %psum.47 = f32[]{:T(128)} all-reduce(f32[]{:T(128)} %fusion.60), channel_id=1, replica_groups=mesh['gx'=16,'gy'=8] {'gx','gy'}, use_global_device_ids=true, to_apply=%region_14.17 | all-reduce | flops 1 | bytes 8 | tf_op jit(solution)/shard_map/psum | solution.py:221
  (296 shorter events, 23.4 us)
Async XLA Ops:
  7.2 57.4 %all-gather.9.cloned.1.call-start = ((), (), s32[]{:S(2)}) async-start(), calls=%async_computation.2 | async-start | bytes 1262080 | tf_op jit(solution)/shard_map/all_gather | solution.py:272
  10.0 7.8 copy-start.3
  10.0 8.7 %copy-start.7 = (f32[1,1,64,128]{3,2,1,0:T(8,128)S(1)}, f32[1,1,64,128]{3,2,1,0:T(8,128)}, u32[]{:S(2)}) copy-start(f32[1,1,64,128]{3,2,1,0:T(8,128)} %param.14) | copy-start | bytes 98308
  10.0 90.8 %all-gather.5.cloned.1.call-start = ((), (), s32[]{:S(2)}) async-start(), calls=%async_computation | async-start | bytes 1418752 | tf_op jit(solution)/shard_map/all_gather | solution.py:270
  19.9 127.2 %all-gather.7.cloned.1.call-start = ((), (), s32[]{:S(2)}) async-start(), calls=%async_computation.1 | async-start | bytes 1575424 | tf_op jit(solution)/shard_map/all_gather | solution.py:271
  20.7 5.4 copy-start.45
  20.7 219.2 %all-gather.11.cloned.1.call-start = ((), (), s32[]{:S(2)}) async-start(), calls=%async_computation.3 | async-start | bytes 2785280 | tf_op jit(solution)/shard_map/all_gather | solution.py:319
  30.4 21.9 %copy-start.4 = (f32[1,1,35,64,128]{4,3,2,1,0:T(8,128)S(1)}, f32[1,1,35,64,128]{4,3,2,1,0:T(8,128)}, u32[]{:S(2)}) copy-start(f32[1,1,35,64,128]{4,3,2,1,0:T(8,128)} %param.13) | copy-start | bytes 3440644
  46.1 10.1 %copy-start.46 = (s32[8,28]{1,0:T(8,128)S(1)}, s32[8,28]{1,0:T(8,128)}, u32[]{:S(2)}) copy-start(s32[8,28]{1,0:T(8,128)} %param.15) | copy-start | bytes 2692
  64.6 87.1 %collective-permute-start.1 = (f32[1,16,18560]{2,0,1:T(1,128)}, f32[1,16,18560]{2,0,1:T(1,128)}, u32[]{:S(2)}, u32[]{:S(2)}) collective-permute-start(f32[1,16,18560]{2,0,1:T(1,128)} %all-gather.9.cloned.1.call-done), channel_id=1, source_target_pairs={{1,0},{2,1},{3,2},{4,3},{5,4},{6,5},{7,6},{9,8},{10,9},{11,10},{12... | collective-permute-start | bytes 3563528 | tf_op jit(solution)/shard_map/ppermute | solution.py:18
  102.6 14.9 %copy-start.6 = (f32[1,1,1,36,64,128]{5,4,3,2,1,0:T(8,128)S(1)}, f32[1,1,1,36,64,128]{5,4,3,2,1,0:T(8,128)}, u32[]{:S(2)}) copy-start(f32[1,1,1,36,64,128]{5,4,3,2,1,0:T(8,128)} %get-tuple-element.259) | copy-start | bytes 3538948
  117.5 2.4 copy-start.1
  117.5 5.5 slice-start
  119.8 3.1 slice-start.1
  119.8 4.7 copy-start.2
  130.2 5.1 copy-start
  135.5 32.8 %copy-start.5 = (f32[1,1,1,36,64,128]{5,4,3,2,1,0:T(8,128)S(1)}, f32[1,1,1,36,64,128]{5,4,3,2,1,0:T(8,128)}, u32[]{:S(2)}) copy-start(f32[1,1,1,36,64,128]{5,4,3,2,1,0:T(8,128)} %get-tuple-element.258) | copy-start | bytes 3538948
  147.0 21.2 %collective-permute-start = (f32[1,16,23168]{2,0,1:T(1,128)}, f32[1,16,23168]{2,0,1:T(1,128)S(1)}, u32[]{:S(2)}, u32[]{:S(2)}) collective-permute-start(f32[1,16,23168]{2,0,1:T(1,128)} %all-gather.7.cloned.1.call-done), channel_id=1, source_target_pairs={{0,1},{1,2},{2,3},{3,4},{4,5},{5,6},{6,7},{8,9},{9,10},{10,11},{11... | collective-permute-start | bytes 4448264 | tf_op jit(solution)/shard_map/ppermute | solution.py:18
  168.3 7.8 slice-start.2
  168.3 7.8 slice-start.4
  168.5 7.6 slice-start.3
  168.5 7.6 slice-start.5
  176.1 9.9 %copy-start.9 = (f32[64,128]{1,0:T(8,128)S(1)}, f32[64,128]{1,0:T(8,128)}, u32[]{:S(2)}) copy-start(f32[64,128]{1,0:T(8,128)} %get-tuple-element.263) | copy-start | bytes 98308
  176.1 9.9 %copy-start.10 = (f32[64,128]{1,0:T(8,128)S(1)}, f32[64,128]{1,0:T(8,128)}, u32[]{:S(2)}) copy-start(f32[64,128]{1,0:T(8,128)} %get-tuple-element.183) | copy-start | bytes 98308
  176.2 9.9 %copy-start.11 = (f32[64,128]{1,0:T(8,128)S(1)}, f32[64,128]{1,0:T(8,128)}, u32[]{:S(2)}) copy-start(f32[64,128]{1,0:T(8,128)} %get-tuple-element.188) | copy-start | bytes 98308
  176.2 9.9 %copy-start.12 = (f32[64,128]{1,0:T(8,128)S(1)}, f32[64,128]{1,0:T(8,128)}, u32[]{:S(2)}) copy-start(f32[64,128]{1,0:T(8,128)} %get-tuple-element.192) | copy-start | bytes 98308
  176.2 9.9 %copy-start.13 = (f32[64,128]{1,0:T(8,128)S(1)}, f32[64,128]{1,0:T(8,128)}, u32[]{:S(2)}) copy-start(f32[64,128]{1,0:T(8,128)} %get-tuple-element.196) | copy-start | bytes 98308
  176.2 9.9 %copy-start.14 = (f32[64,128]{1,0:T(8,128)S(1)}, f32[64,128]{1,0:T(8,128)}, u32[]{:S(2)}) copy-start(f32[64,128]{1,0:T(8,128)} %get-tuple-element.200) | copy-start | bytes 98308
  176.2 9.9 %copy-start.15 = (f32[64,128]{1,0:T(8,128)S(1)}, f32[64,128]{1,0:T(8,128)}, u32[]{:S(2)}) copy-start(f32[64,128]{1,0:T(8,128)} %get-tuple-element.204) | copy-start | bytes 98308
  176.2 9.9 %copy-start.16 = (f32[64,128]{1,0:T(8,128)S(1)}, f32[64,128]{1,0:T(8,128)}, u32[]{:S(2)}) copy-start(f32[64,128]{1,0:T(8,128)} %get-tuple-element.208) | copy-start | bytes 98308
  176.2 9.9 %copy-start.17 = (f32[64,128]{1,0:T(8,128)S(1)}, f32[64,128]{1,0:T(8,128)}, u32[]{:S(2)}) copy-start(f32[64,128]{1,0:T(8,128)} %get-tuple-element.212) | copy-start | bytes 98308
  176.2 9.9 %copy-start.18 = (f32[64,128]{1,0:T(8,128)S(1)}, f32[64,128]{1,0:T(8,128)}, u32[]{:S(2)}) copy-start(f32[64,128]{1,0:T(8,128)} %get-tuple-element.216) | copy-start | bytes 98308
  176.2 9.9 %copy-start.19 = (f32[64,128]{1,0:T(8,128)S(1)}, f32[64,128]{1,0:T(8,128)}, u32[]{:S(2)}) copy-start(f32[64,128]{1,0:T(8,128)} %get-tuple-element.220) | copy-start | bytes 98308
  176.2 9.9 %copy-start.20 = (f32[64,128]{1,0:T(8,128)S(1)}, f32[64,128]{1,0:T(8,128)}, u32[]{:S(2)}) copy-start(f32[64,128]{1,0:T(8,128)} %get-tuple-element.224) | copy-start | bytes 98308
  176.3 9.9 %copy-start.21 = (f32[64,128]{1,0:T(8,128)S(1)}, f32[64,128]{1,0:T(8,128)}, u32[]{:S(2)}) copy-start(f32[64,128]{1,0:T(8,128)} %get-tuple-element.228) | copy-start | bytes 98308
  176.3 9.9 %copy-start.22 = (f32[64,128]{1,0:T(8,128)S(1)}, f32[64,128]{1,0:T(8,128)}, u32[]{:S(2)}) copy-start(f32[64,128]{1,0:T(8,128)} %get-tuple-element.232) | copy-start | bytes 98308
  176.3 9.9 %copy-start.23 = (f32[64,128]{1,0:T(8,128)S(1)}, f32[64,128]{1,0:T(8,128)}, u32[]{:S(2)}) copy-start(f32[64,128]{1,0:T(8,128)} %get-tuple-element.236) | copy-start | bytes 98308
  176.3 9.9 %copy-start.24 = (f32[64,128]{1,0:T(8,128)S(1)}, f32[64,128]{1,0:T(8,128)}, u32[]{:S(2)}) copy-start(f32[64,128]{1,0:T(8,128)} %get-tuple-element.240) | copy-start | bytes 98308
  176.3 9.9 %copy-start.25 = (f32[64,128]{1,0:T(8,128)S(1)}, f32[64,128]{1,0:T(8,128)}, u32[]{:S(2)}) copy-start(f32[64,128]{1,0:T(8,128)} %get-tuple-element.244) | copy-start | bytes 98308
  176.3 9.9 %copy-start.26 = (f32[64,128]{1,0:T(8,128)S(1)}, f32[64,128]{1,0:T(8,128)}, u32[]{:S(2)}) copy-start(f32[64,128]{1,0:T(8,128)} %get-tuple-element.248) | copy-start | bytes 98308
  176.3 9.9 %copy-start.27 = (f32[64,128]{1,0:T(8,128)S(1)}, f32[64,128]{1,0:T(8,128)}, u32[]{:S(2)}) copy-start(f32[64,128]{1,0:T(8,128)} %get-tuple-element.184) | copy-start | bytes 98308
  176.3 9.9 %copy-start.29 = (f32[64,128]{1,0:T(8,128)S(1)}, f32[64,128]{1,0:T(8,128)}, u32[]{:S(2)}) copy-start(f32[64,128]{1,0:T(8,128)} %get-tuple-element.297) | copy-start | bytes 98308
  176.3 9.9 %copy-start.30 = (f32[64,128]{1,0:T(8,128)S(1)}, f32[64,128]{1,0:T(8,128)}, u32[]{:S(2)}) copy-start(f32[64,128]{1,0:T(8,128)} %get-tuple-element.298) | copy-start | bytes 98308
  176.3 9.9 %copy-start.31 = (f32[64,128]{1,0:T(8,128)S(1)}, f32[64,128]{1,0:T(8,128)}, u32[]{:S(2)}) copy-start(f32[64,128]{1,0:T(8,128)} %get-tuple-element.281) | copy-start | bytes 98308
  176.4 9.9 %copy-start.32 = (f32[64,128]{1,0:T(8,128)S(1)}, f32[64,128]{1,0:T(8,128)}, u32[]{:S(2)}) copy-start(f32[64,128]{1,0:T(8,128)} %get-tuple-element.282) | copy-start | bytes 98308
  176.4 9.9 %copy-start.33 = (f32[64,128]{1,0:T(8,128)S(1)}, f32[64,128]{1,0:T(8,128)}, u32[]{:S(2)}) copy-start(f32[64,128]{1,0:T(8,128)} %get-tuple-element.283) | copy-start | bytes 98308
  176.4 9.9 %copy-start.34 = (f32[64,128]{1,0:T(8,128)S(1)}, f32[64,128]{1,0:T(8,128)}, u32[]{:S(2)}) copy-start(f32[64,128]{1,0:T(8,128)} %get-tuple-element.284) | copy-start | bytes 98308
  176.4 9.9 %copy-start.35 = (f32[64,128]{1,0:T(8,128)S(1)}, f32[64,128]{1,0:T(8,128)}, u32[]{:S(2)}) copy-start(f32[64,128]{1,0:T(8,128)} %get-tuple-element.285) | copy-start | bytes 98308
  176.4 9.9 %copy-start.36 = (f32[64,128]{1,0:T(8,128)S(1)}, f32[64,128]{1,0:T(8,128)}, u32[]{:S(2)}) copy-start(f32[64,128]{1,0:T(8,128)} %get-tuple-element.286) | copy-start | bytes 98308
  176.4 9.9 %copy-start.37 = (f32[64,128]{1,0:T(8,128)S(1)}, f32[64,128]{1,0:T(8,128)}, u32[]{:S(2)}) copy-start(f32[64,128]{1,0:T(8,128)} %get-tuple-element.287) | copy-start | bytes 98308
  176.4 9.9 %copy-start.38 = (f32[64,128]{1,0:T(8,128)S(1)}, f32[64,128]{1,0:T(8,128)}, u32[]{:S(2)}) copy-start(f32[64,128]{1,0:T(8,128)} %get-tuple-element.288) | copy-start | bytes 98308
  176.4 9.9 %copy-start.39 = (f32[64,128]{1,0:T(8,128)S(1)}, f32[64,128]{1,0:T(8,128)}, u32[]{:S(2)}) copy-start(f32[64,128]{1,0:T(8,128)} %get-tuple-element.289) | copy-start | bytes 98308
  176.4 9.9 %copy-start.40 = (f32[64,128]{1,0:T(8,128)S(1)}, f32[64,128]{1,0:T(8,128)}, u32[]{:S(2)}) copy-start(f32[64,128]{1,0:T(8,128)} %get-tuple-element.290) | copy-start | bytes 98308
  176.4 9.9 %copy-start.41 = (f32[64,128]{1,0:T(8,128)S(1)}, f32[64,128]{1,0:T(8,128)}, u32[]{:S(2)}) copy-start(f32[64,128]{1,0:T(8,128)} %get-tuple-element.291) | copy-start | bytes 98308
  176.5 9.9 %copy-start.42 = (f32[64,128]{1,0:T(8,128)S(1)}, f32[64,128]{1,0:T(8,128)}, u32[]{:S(2)}) copy-start(f32[64,128]{1,0:T(8,128)} %get-tuple-element.292) | copy-start | bytes 98308
  176.5 9.9 %copy-start.43 = (f32[64,128]{1,0:T(8,128)S(1)}, f32[64,128]{1,0:T(8,128)}, u32[]{:S(2)}) copy-start(f32[64,128]{1,0:T(8,128)} %get-tuple-element.293) | copy-start | bytes 98308
  189.8 4.0 copy-start.44
  190.2 2.2 copy-start.8
  242.6 24.6 %collective-permute-start.3 = (f32[1,2,128]{2,1,0:T(2,128)S(1)}, f32[1,2,128]{2,1,0:T(2,128)S(1)}, u32[]{:S(2)}, u32[]{:S(2)}) collective-permute-start(f32[1,2,128]{2,1,0:T(2,128)S(1)} %bitcast.731), channel_id=1, source_target_pairs={{0,1},{1,2},{2,3},{3,4},{4,5},{5,6},{6,7},{8,9},{9,10},{10,11},{11... | collective-permute-start | bytes 3080 | tf_op jit(solution)/shard_map/ppermute | solution.py:18
  246.6 36.6 %collective-permute-start.2 = (f32[1,2,128]{2,1,0:T(2,128)S(1)}, f32[1,2,128]{2,1,0:T(2,128)S(1)}, u32[]{:S(2)}, u32[]{:S(2)}) collective-permute-start(f32[1,2,128]{2,1,0:T(2,128)S(1)} %bitcast.730), channel_id=1, source_target_pairs={{1,0},{2,1},{3,2},{4,3},{5,4},{6,5},{7,6},{9,8},{10,9},{11,10},{12... | collective-permute-start | bytes 3080 | tf_op jit(solution)/shard_map/ppermute | solution.py:18
  465.5 11.5 %collective-permute-start.5 = (f32[1,2,128]{2,1,0:T(2,128)S(1)}, f32[1,2,128]{2,1,0:T(2,128)S(1)}, u32[]{:S(2)}, u32[]{:S(2)}) collective-permute-start(f32[1,2,128]{2,1,0:T(2,128)S(1)} %bitcast.733), channel_id=1, source_target_pairs={{0,1},{1,2},{2,3},{3,4},{4,5},{5,6},{6,7},{8,9},{9,10},{10,11},{11... | collective-permute-start | bytes 3080 | tf_op jit(solution)/shard_map/ppermute | solution.py:18
  474.6 19.0 %collective-permute-start.4 = (f32[1,2,128]{2,1,0:T(2,128)S(1)}, f32[1,2,128]{2,1,0:T(2,128)S(1)}, u32[]{:S(2)}, u32[]{:S(2)}) collective-permute-start(f32[1,2,128]{2,1,0:T(2,128)S(1)} %bitcast.729), channel_id=1, source_target_pairs={{1,0},{2,1},{3,2},{4,3},{5,4},{6,5},{7,6},{9,8},{10,9},{11,10},{12... | collective-permute-start | bytes 3080 | tf_op jit(solution)/shard_map/ppermute | solution.py:18
  670.1 11.4 %collective-permute-start.6 = (f32[1,2,128]{2,1,0:T(2,128)S(1)}, f32[1,2,128]{2,1,0:T(2,128)S(1)}, u32[]{:S(2)}, u32[]{:S(2)}) collective-permute-start(f32[1,2,128]{2,1,0:T(2,128)S(1)} %bitcast.734), channel_id=1, source_target_pairs={{1,0},{2,1},{3,2},{4,3},{5,4},{6,5},{7,6},{9,8},{10,9},{11,10},{12... | collective-permute-start | bytes 3080 | tf_op jit(solution)/shard_map/ppermute | solution.py:18
  678.1 20.5 %collective-permute-start.7 = (f32[1,2,128]{2,1,0:T(2,128)S(1)}, f32[1,2,128]{2,1,0:T(2,128)S(1)}, u32[]{:S(2)}, u32[]{:S(2)}) collective-permute-start(f32[1,2,128]{2,1,0:T(2,128)S(1)} %bitcast.732), channel_id=1, source_target_pairs={{0,1},{1,2},{2,3},{3,4},{4,5},{5,6},{6,7},{8,9},{9,10},{10,11},{11... | collective-permute-start | bytes 3080 | tf_op jit(solution)/shard_map/ppermute | solution.py:18
  (1 other events, 0.7 us)
Sparse Core Ops, SparseCore 0:
  10.1 45.1 all-gather.8
  58.1 42.7 all-gather.4
  103.0 43.9 all-gather.6
  193.9 46.0 all-gather.10
where the time goes:
time: 798 us; the launch traced here: 797 us
  blocking collectives  499 us (63%)
  local copies, waits for them, and re-layouts  101 us (13%)
  waiting for transfers between devices  81.1 us (10%)
  other arithmetic  45.1 us (6%)
  starting transfers between devices  36.4 us (5%)
  between operations  33.6 us (4%)
    psum x3, blocking collectives, squares(): return lax.psum(jnp.sum(residual * residual), ('gx', 'gy'))  207 us
    psum x2, blocking collectives, solve(): lax.psum(jnp.sum(direction * image_field), ('gx', 'gy'))  145 us
    all_gather x3, blocking collectives, exchange_edges(): lax.all_gather(from_above, 'gx', axis=1, tiled=True)  50.7 us
    all_gather x3, blocking collectives, exchange_edges(): lax.all_gather(side_cols, 'gx', axis=1, tiled=True)  48.3 us
    all_gather x3, blocking collectives, exchange_edges(): lax.all_gather(from_below, 'gx', axis=1, tiled=True)  48.2 us
    ppermute x8, starting transfers between devices, passed_along(): lax.ppermute(value, axis, [(source, source + steps) for source in range(l...  36.3 us
    all_gather x1, waiting for transfers between devices, body(): lax.all_gather(side_cols, 'gx', axis=1, tiled=True)  32.6 us
    all_gather x1, waiting for transfers between devices, body(): band_fields = lax.all_gather(packed, 'gx', axis=1, tiled=True)  31.2 us
  transfers between devices with their start and end apart: 12, of which 4 were waited for; matrix products, arithmetic and copies ran while one was open for 13% of the time, Pallas kernels for 0%

commit v1 on v0

--- a/solution.py
+++ b/solution.py
@@ -316,7 +316,12 @@
     inverse_row = lax.dynamic_index_in_dim(inverse, band_row, 0, keepdims=False)
     source_slot = jnp.take(inverse_row, jnp.maximum(own_tropic, 0), axis=0)
     packed = jnp.concatenate([column_forcing[:, :, None], weights], axis=2)
-    band_fields = lax.all_gather(packed, "gx", axis=1, tiled=True)
+    ring = [packed]
+    for hop in range(15):
+        ring.append(lax.ppermute(ring[-1], "gx", [(dev, (dev + 1) % 16) for dev in range(16)]))
+    band_fields = jnp.roll(
+        jnp.concatenate(ring[::-1], axis=1), (lax.axis_index("gx") + 1) * ring[0].shape[1], axis=1
+    )
     moved = jnp.where(in_use[..., None], picked(band_fields, source_slot), 0.0)
     tropic_inverse = inverse_map(tropic_list, row_width)
     tropic_ids = jnp.full((1, tropic_count), band_row, jnp.int32)

time: 798 us -> 894 us (1.12)
  waiting for transfers between devices: 81.1 us -> 157 us
  starting transfers between devices: 36.4 us -> 51.2 us
    ppermute x0 -> x15, waiting for transfers between devices: none -> 108 us  [body(): lax.ppermute(ring[-1], 'gx', [(dev, (dev + 1) % 16) for dev in range(16)])]
    all_gather x1 -> x0, waiting for transfers between devices: 31.2 us -> none  [body(): band_fields = lax.all_gather(packed, 'gx', axis=1, tiled=True)]
    ppermute x8, starting transfers between devices: 36.3 us -> 49.8 us  [passed_along(): lax.ppermute(value, axis, [(source, source + steps) for source in range(l...]
  transfers between devices with their start and end apart: 12 -> 26, of which waited for: 4 -> 17; matrix products, arithmetic and copies ran while one was open for 13% -> 12% of each run, Pallas kernels for 0% -> 0%
where the time goes in v1:
time: 894 us; the launch traced here: 886 us
  blocking collectives  501 us (56%)
  waiting for transfers between devices  157 us (18%)
  local copies, waits for them, and re-layouts  97.1 us (11%)
  starting transfers between devices  51.2 us (6%)
  other arithmetic  46 us (5%)
  between operations  33.9 us (4%)
    psum x3, blocking collectives, squares(): return lax.psum(jnp.sum(residual * residual), ('gx', 'gy'))  206 us
    psum x2, blocking collectives, solve(): lax.psum(jnp.sum(direction * image_field), ('gx', 'gy'))  147 us
    ppermute x15, waiting for transfers between devices, body(): lax.ppermute(ring[-1], 'gx', [(dev, (dev + 1) % 16) for dev in range(16)])  108 us
    all_gather x3, blocking collectives, exchange_edges(): lax.all_gather(from_below, 'gx', axis=1, tiled=True)  51.3 us
    ppermute x8, starting transfers between devices, passed_along(): lax.ppermute(value, axis, [(source, source + steps) for source in range(l...  49.8 us
    all_gather x3, blocking collectives, exchange_edges(): lax.all_gather(side_cols, 'gx', axis=1, tiled=True)  48.9 us
    all_gather x3, blocking collectives, exchange_edges(): lax.all_gather(from_above, 'gx', axis=1, tiled=True)  47.4 us
    all_gather x1, waiting for transfers between devices, body(): lax.all_gather(side_cols, 'gx', axis=1, tiled=True)  32 us
  transfers between devices with their start and end apart: 26, of which 17 were waited for; matrix products, arithmetic and copies ran while one was open for 12% of the time, Pallas kernels for 0%

profile of v1, /device:TPU:1, one launch (start us, length us, event | category | flops | bytes accessed | tf_op | source)
XLA Modules:
  0.0 886.1 jit_solution(13852805945445001443)
XLA Ops:
  7.9 1.4 fusion.178
  10.1 7.6 slice_reduce_fusion
  20.7 5.3 constant_dynamic-update-slice_fusion.1
  30.2 6.4 scatter_fusion
  36.6 5.7 fusion.192
  46.2 1.6 fusion.179
  52.6 1.5 multiply_subtract_fusion.4
  55.9 5.7 fusion.191
  65.0 3.9 collective-permute-start.1
  68.8 32.0 %all-gather.4.cloned.1.call-done = f32[1,16,20864]{2,0,1:T(1,128)} async-done(((f32[1,1,20864]{2,0,1:T(1,128)}), f32[1,16,20864]{2,0,1:T(1,128)}) %all-gather.4.cloned.1.call-update) | async-done | bytes 1335312 | tf_op jit(solution)/shard_map/all_gather | solution.py:270
  100.9 1.4 copy.184
  102.6 6.8 concatenate.619
  109.6 6.9 concatenate.618
  116.5 1.0 broadcast_in_dim_broadcast_in_dim_reshape.8
  118.2 1.7 copy-done.1
  119.9 3.1 constant_dynamic-update-slice_fusion
  123.0 1.6 copy-done.2
  124.6 5.7 multiply_subtract_fusion
  130.3 3.8 slice.756
  134.2 1.2 copy-done
  135.7 9.9 %slice_multiply_fusion = (f32[1,1,4,36,64,1]{5,4,3,2,1,0:T(8,128)}, f32[1,1,4,36,64,1]{5,4,3,2,1,0:T(8,128)}) fusion(f32[1,1,4,36,64,129]{5,4,3,2,1,0:T(8,128)} %copy-done, f32[]{:T(128)} %bitcast.22, f32[]{:T(128)} %bitcast.21), kind=kLoop, calls=%fused_computation.25 | loop fusion | flops 18432 | bytes 147464 | tf_op jit(solution)/shard_map/mul | solution.py:72
  145.5 1.5 all-gather.6.cloned.1.call-done
  147.1 4.6 collective-permute-start
  151.7 1.0 broadcast_select_fusion.3
  152.7 15.5 %collective-permute-done = f32[1,16,23168]{2,0,1:T(1,128)S(1)} collective-permute-done((f32[1,16,23168]{2,0,1:T(1,128)}, f32[1,16,23168]{2,0,1:T(1,128)S(1)}, u32[]{:S(2)}, u32[]{:S(2)}) %collective-permute-start) | collective-permute-done | bytes 1482784 | tf_op jit(solution)/shard_map/ppermute | solution.py:18
  168.6 4.6 multiply_subtract_fusion.1
  173.2 2.9 slice.762
  176.6 10.3 %fusion.1 = f32[1,1,4,36,64,128]{5,4,3,2,1,0:T(8,128)S(1)} fusion(f32[1,1,4,36,64,128]{5,4,3,2,1,0:T(8,128)S(1)} %bitcast.677, f32[1,1,4,36,64,1]{5,4,3,2,1,0:T(8,128)} %get-tuple-element.261, f32[1,1,4,36,64,127]{5,4,3,2,1,0:T(8,128)S(1)} %bitcast.679, f32[1,1,4,36,64,1]{5,4,3,2,1,0:T(8,128)} %get-tuple-element.260, ...), kind=kLoop, calls=%fused_computation.29 | loop fusion | flops 9437184 | bytes 18984960 | tf_op jit(solution)/shard_map/sub | solution.py:114
  187.2 3.0 constant_dynamic-update-slice_fusion.37
  192.6 6.6 collective-permute-done.2
  199.2 7.5 collective-permute-done.3
  206.6 7.5 collective-permute-done.4
  214.3 11.2 %scatter_fusion.1 = s32[8,29]{1,0:T(8,128)S(1)} fusion(s32[8,29]{1,0:T(8,128)S(1)} %broadcast.10949.clone.1, s32[256]{0:T(256)S(1)} %reshape.20049, s32[256]{0:T(256)S(1)} %reshape.20051), kind=kCustom, calls=%fused_computation.19 | custom fusion | bytes 5120 | tf_op jit(solution)/shard_map/scatter | solution.py:30
  228.1 6.8 collective-permute-done.6
  235.0 7.7 collective-permute-done.7
  242.6 8.7 collective-permute-done.8
  251.4 8.9 collective-permute-done.9
  260.2 7.9 collective-permute-done.10
  268.2 7.5 collective-permute-done.11
  275.7 7.5 collective-permute-done.12
  283.2 7.5 collective-permute-done.13
  290.9 7.4 collective-permute-done.14
  298.4 7.6 collective-permute-done.15
  306.1 8.7 collective-permute-done.16
  316.7 19.6 %collective-permute-start.18 = (f32[1,2,128]{2,1,0:T(2,128)S(1)}, f32[1,2,128]{2,1,0:T(2,128)S(1)}, u32[]{:S(2)}, u32[]{:S(2)}) collective-permute-start(f32[1,2,128]{2,1,0:T(2,128)S(1)} %bitcast.729), channel_id=1, source_target_pairs={{0,1},{1,2},{2,3},{3,4},{4,5},{5,6},{6,7},{8,9},{9,10},{10,11},{11... | collective-permute-start | bytes 3080 | tf_op jit(solution)/shard_map/ppermute | solution.py:18
  336.3 1.9 collective-permute-start.17
  338.3 14.8 %all_gather.39 = f32[1,32,128]{2,0,1:T(1,128)S(1)} all-gather(f32[1,2,128]{2,0,1:T(1,128)S(1)} %bitcast.716), channel_id=1, replica_groups=mesh['gx'=16,'gy'=8] {'gx'}, dimensions={1}, use_global_device_ids=true | all-gather | bytes 17408 | tf_op jit(solution)/shard_map/all_gather | solution.py:198
  354.7 17.9 %all_gather.41 = f32[1,32,128]{2,0,1:T(1,128)S(1)} all-gather(f32[1,2,128]{2,0,1:T(1,128)S(1)} %bitcast.722), channel_id=1, replica_groups=mesh['gx'=16,'gy'=8] {'gx'}, dimensions={1}, use_global_device_ids=true | all-gather | bytes 17408 | tf_op jit(solution)/shard_map/all_gather | solution.py:199
  372.6 15.2 %all_gather.40 = f32[1,32,128]{2,0,1:T(1,128)S(1)} all-gather(f32[1,2,128]{2,0,1:T(1,128)S(1)} %bitcast.721), channel_id=1, replica_groups=mesh['gx'=16,'gy'=8] {'gx'}, dimensions={1}, use_global_device_ids=true | all-gather | bytes 17408 | tf_op jit(solution)/shard_map/all_gather | solution.py:200
  389.8 80.8 %all-reduce.4 = (f32[]{:T(128)}, f32[]{:T(128)}) all-reduce(f32[]{:T(128)} %get-tuple-element.130, f32[]{:T(128)} %get-tuple-element.129), channel_id=1, replica_groups=mesh['gx'=16,'gy'=8] {'gx','gy'}, use_global_device_ids=true, to_apply=%region_3.5 | all-reduce | flops 2 | bytes 16 | tf_op jit(solution)/shard_map/psum | solution.py:211
  472.6 62.7 %psum.44 = f32[]{:T(128)} all-reduce(f32[]{:T(128)} %get-tuple-element.143), channel_id=1, replica_groups=mesh['gx'=16,'gy'=8] {'gx','gy'}, use_global_device_ids=true, to_apply=%region_8.11 | all-reduce | flops 1 | bytes 8 | tf_op jit(solution)/shard_map/psum | solution.py:211
  536.9 17.1 %all_gather.42 = f32[1,32,128]{2,0,1:T(1,128)S(1)} all-gather(f32[1,2,128]{2,0,1:T(1,128)S(1)} %bitcast.717), channel_id=1, replica_groups=mesh['gx'=16,'gy'=8] {'gx'}, dimensions={1}, use_global_device_ids=true | all-gather | bytes 17408 | tf_op jit(solution)/shard_map/all_gather | solution.py:198
  555.1 7.3 collective-permute-start.20
  562.4 2.3 collective-permute-start.19
  565.2 17.0 %all_gather.44 = f32[1,32,128]{2,0,1:T(1,128)S(1)} all-gather(f32[1,2,128]{2,0,1:T(1,128)S(1)} %bitcast.724), channel_id=1, replica_groups=mesh['gx'=16,'gy'=8] {'gx'}, dimensions={1}, use_global_device_ids=true | all-gather | bytes 17408 | tf_op jit(solution)/shard_map/all_gather | solution.py:199
  582.9 15.9 %all_gather.43 = f32[1,32,128]{2,0,1:T(1,128)S(1)} all-gather(f32[1,2,128]{2,0,1:T(1,128)S(1)} %bitcast.723), channel_id=1, replica_groups=mesh['gx'=16,'gy'=8] {'gx'}, dimensions={1}, use_global_device_ids=true | all-gather | bytes 17408 | tf_op jit(solution)/shard_map/all_gather | solution.py:200
  600.1 74.5 %psum.45 = f32[]{:T(128)} all-reduce(f32[]{:T(128)} %get-tuple-element.141), channel_id=1, replica_groups=mesh['gx'=16,'gy'=8] {'gx','gy'}, use_global_device_ids=true, to_apply=%region_10.13 | all-reduce | flops 1 | bytes 8 | tf_op jit(solution)/shard_map/psum | solution.py:221
  676.6 62.5 %psum.46 = f32[]{:T(128)} all-reduce(f32[]{:T(128)} %multiply_reduce_fusion), channel_id=1, replica_groups=mesh['gx'=16,'gy'=8] {'gx','gy'}, use_global_device_ids=true, to_apply=%region_12.15 | all-reduce | flops 1 | bytes 8 | tf_op jit(solution)/shard_map/psum | solution.py:211
  740.9 17.1 %all_gather.45 = f32[1,32,128]{2,0,1:T(1,128)S(1)} all-gather(f32[1,2,128]{2,0,1:T(1,128)S(1)} %bitcast.718), channel_id=1, replica_groups=mesh['gx'=16,'gy'=8] {'gx'}, dimensions={1}, use_global_device_ids=true | all-gather | bytes 17408 | tf_op jit(solution)/shard_map/all_gather | solution.py:198
  759.4 8.2 collective-permute-start.21
  767.8 1.9 collective-permute-start.22
  769.8 16.4 %all_gather.46 = f32[1,32,128]{2,0,1:T(1,128)S(1)} all-gather(f32[1,2,128]{2,0,1:T(1,128)S(1)} %bitcast.726), channel_id=1, replica_groups=mesh['gx'=16,'gy'=8] {'gx'}, dimensions={1}, use_global_device_ids=true | all-gather | bytes 17408 | tf_op jit(solution)/shard_map/all_gather | solution.py:200
  786.8 16.4 %all_gather.47 = f32[1,32,128]{2,0,1:T(1,128)S(1)} all-gather(f32[1,2,128]{2,0,1:T(1,128)S(1)} %bitcast.725), channel_id=1, replica_groups=mesh['gx'=16,'gy'=8] {'gx'}, dimensions={1}, use_global_device_ids=true | all-gather | bytes 17408 | tf_op jit(solution)/shard_map/all_gather | solution.py:199
  804.5 72.9 %psum.47 = f32[]{:T(128)} all-reduce(f32[]{:T(128)} %fusion.60), channel_id=1, replica_groups=mesh['gx'=16,'gy'=8] {'gx','gy'}, use_global_device_ids=true, to_apply=%region_14.17 | all-reduce | flops 1 | bytes 8 | tf_op jit(solution)/shard_map/psum | solution.py:221
  (362 shorter events, 33.4 us)
Async XLA Ops:
  7.2 57.8 %all-gather.8.cloned.1.call-start = ((), (), s32[]{:S(2)}) async-start(), calls=%async_computation.2 | async-start | bytes 1262080 | tf_op jit(solution)/shard_map/all_gather | solution.py:272
  10.0 90.8 %all-gather.4.cloned.1.call-start = ((), (), s32[]{:S(2)}) async-start(), calls=%async_computation | async-start | bytes 1418752 | tf_op jit(solution)/shard_map/all_gather | solution.py:270
  19.9 127.2 %all-gather.6.cloned.1.call-start = ((), (), s32[]{:S(2)}) async-start(), calls=%async_computation.1 | async-start | bytes 1575424 | tf_op jit(solution)/shard_map/all_gather | solution.py:271
  30.2 21.8 %copy-start.4 = (f32[1,1,35,64,128]{4,3,2,1,0:T(8,128)S(1)}, f32[1,1,35,64,128]{4,3,2,1,0:T(8,128)}, u32[]{:S(2)}) copy-start(f32[1,1,35,64,128]{4,3,2,1,0:T(8,128)} %param.13) | copy-start | bytes 3440644
  46.2 17.9 %copy-start.43 = (s32[8,32]{1,0:T(8,128)S(1)}, s32[8,32]{1,0:T(8,128)}, u32[]{:S(2)}) copy-start(s32[8,32]{1,0:T(8,128)} %param.17) | copy-start | bytes 3076
  65.0 86.8 %collective-permute-start.1 = (f32[1,16,18560]{2,0,1:T(1,128)}, f32[1,16,18560]{2,0,1:T(1,128)}, u32[]{:S(2)}, u32[]{:S(2)}) collective-permute-start(f32[1,16,18560]{2,0,1:T(1,128)} %all-gather.8.cloned.1.call-done), channel_id=1, source_target_pairs={{1,0},{2,1},{3,2},{4,3},{5,4},{6,5},{7,6},{9,8},{10,9},{11,10},{12... | collective-permute-start | bytes 3563528 | tf_op jit(solution)/shard_map/ppermute | solution.py:18
  102.6 14.9 %copy-start.6 = (f32[1,1,1,36,64,128]{5,4,3,2,1,0:T(8,128)S(1)}, f32[1,1,1,36,64,128]{5,4,3,2,1,0:T(8,128)}, u32[]{:S(2)}) copy-start(f32[1,1,1,36,64,128]{5,4,3,2,1,0:T(8,128)} %get-tuple-element.267) | copy-start | bytes 3538948
  135.7 32.7 %copy-start.5 = (f32[1,1,1,36,64,128]{5,4,3,2,1,0:T(8,128)S(1)}, f32[1,1,1,36,64,128]{5,4,3,2,1,0:T(8,128)}, u32[]{:S(2)}) copy-start(f32[1,1,1,36,64,128]{5,4,3,2,1,0:T(8,128)} %get-tuple-element.266) | copy-start | bytes 3538948
  147.1 21.2 %collective-permute-start = (f32[1,16,23168]{2,0,1:T(1,128)}, f32[1,16,23168]{2,0,1:T(1,128)S(1)}, u32[]{:S(2)}, u32[]{:S(2)}) collective-permute-start(f32[1,16,23168]{2,0,1:T(1,128)} %all-gather.6.cloned.1.call-done), channel_id=1, source_target_pairs={{0,1},{1,2},{2,3},{3,4},{4,5},{5,6},{6,7},{8,9},{9,10},{10,11},{11... | collective-permute-start | bytes 4448264 | tf_op jit(solution)/shard_map/ppermute | solution.py:18
  176.2 10.6 %copy-start.9 = (f32[64,128]{1,0:T(8,128)S(1)}, f32[64,128]{1,0:T(8,128)}, u32[]{:S(2)}) copy-start(f32[64,128]{1,0:T(8,128)} %get-tuple-element.271) | copy-start | bytes 98308
  176.2 10.6 %copy-start.10 = (f32[64,128]{1,0:T(8,128)S(1)}, f32[64,128]{1,0:T(8,128)}, u32[]{:S(2)}) copy-start(f32[64,128]{1,0:T(8,128)} %get-tuple-element.191) | copy-start | bytes 98308
  176.2 10.6 %copy-start.11 = (f32[64,128]{1,0:T(8,128)S(1)}, f32[64,128]{1,0:T(8,128)}, u32[]{:S(2)}) copy-start(f32[64,128]{1,0:T(8,128)} %get-tuple-element.196) | copy-start | bytes 98308
  176.2 10.6 %copy-start.12 = (f32[64,128]{1,0:T(8,128)S(1)}, f32[64,128]{1,0:T(8,128)}, u32[]{:S(2)}) copy-start(f32[64,128]{1,0:T(8,128)} %get-tuple-element.200) | copy-start | bytes 98308
  176.3 10.6 %copy-start.13 = (f32[64,128]{1,0:T(8,128)S(1)}, f32[64,128]{1,0:T(8,128)}, u32[]{:S(2)}) copy-start(f32[64,128]{1,0:T(8,128)} %get-tuple-element.204) | copy-start | bytes 98308
  176.3 10.6 %copy-start.14 = (f32[64,128]{1,0:T(8,128)S(1)}, f32[64,128]{1,0:T(8,128)}, u32[]{:S(2)}) copy-start(f32[64,128]{1,0:T(8,128)} %get-tuple-element.208) | copy-start | bytes 98308
  176.3 10.6 %copy-start.15 = (f32[64,128]{1,0:T(8,128)S(1)}, f32[64,128]{1,0:T(8,128)}, u32[]{:S(2)}) copy-start(f32[64,128]{1,0:T(8,128)} %get-tuple-element.212) | copy-start | bytes 98308
  176.3 10.6 %copy-start.16 = (f32[64,128]{1,0:T(8,128)S(1)}, f32[64,128]{1,0:T(8,128)}, u32[]{:S(2)}) copy-start(f32[64,128]{1,0:T(8,128)} %get-tuple-element.216) | copy-start | bytes 98308
  176.3 10.6 %copy-start.17 = (f32[64,128]{1,0:T(8,128)S(1)}, f32[64,128]{1,0:T(8,128)}, u32[]{:S(2)}) copy-start(f32[64,128]{1,0:T(8,128)} %get-tuple-element.220) | copy-start | bytes 98308
  176.3 10.6 %copy-start.18 = (f32[64,128]{1,0:T(8,128)S(1)}, f32[64,128]{1,0:T(8,128)}, u32[]{:S(2)}) copy-start(f32[64,128]{1,0:T(8,128)} %get-tuple-element.224) | copy-start | bytes 98308
  176.3 10.6 %copy-start.19 = (f32[64,128]{1,0:T(8,128)S(1)}, f32[64,128]{1,0:T(8,128)}, u32[]{:S(2)}) copy-start(f32[64,128]{1,0:T(8,128)} %get-tuple-element.228) | copy-start | bytes 98308
  176.3 10.6 %copy-start.20 = (f32[64,128]{1,0:T(8,128)S(1)}, f32[64,128]{1,0:T(8,128)}, u32[]{:S(2)}) copy-start(f32[64,128]{1,0:T(8,128)} %get-tuple-element.232) | copy-start | bytes 98308
  176.3 10.6 %copy-start.21 = (f32[64,128]{1,0:T(8,128)S(1)}, f32[64,128]{1,0:T(8,128)}, u32[]{:S(2)}) copy-start(f32[64,128]{1,0:T(8,128)} %get-tuple-element.236) | copy-start | bytes 98308
  176.3 10.6 %copy-start.22 = (f32[64,128]{1,0:T(8,128)S(1)}, f32[64,128]{1,0:T(8,128)}, u32[]{:S(2)}) copy-start(f32[64,128]{1,0:T(8,128)} %get-tuple-element.240) | copy-start | bytes 98308
  176.4 10.6 %copy-start.23 = (f32[64,128]{1,0:T(8,128)S(1)}, f32[64,128]{1,0:T(8,128)}, u32[]{:S(2)}) copy-start(f32[64,128]{1,0:T(8,128)} %get-tuple-element.244) | copy-start | bytes 98308
  176.4 10.6 %copy-start.24 = (f32[64,128]{1,0:T(8,128)S(1)}, f32[64,128]{1,0:T(8,128)}, u32[]{:S(2)}) copy-start(f32[64,128]{1,0:T(8,128)} %get-tuple-element.248) | copy-start | bytes 98308
  176.4 10.6 %copy-start.25 = (f32[64,128]{1,0:T(8,128)S(1)}, f32[64,128]{1,0:T(8,128)}, u32[]{:S(2)}) copy-start(f32[64,128]{1,0:T(8,128)} %get-tuple-element.252) | copy-start | bytes 98308
  176.4 10.6 %copy-start.26 = (f32[64,128]{1,0:T(8,128)S(1)}, f32[64,128]{1,0:T(8,128)}, u32[]{:S(2)}) copy-start(f32[64,128]{1,0:T(8,128)} %get-tuple-element.256) | copy-start | bytes 98308
  176.4 10.6 %copy-start.27 = (f32[64,128]{1,0:T(8,128)S(1)}, f32[64,128]{1,0:T(8,128)}, u32[]{:S(2)}) copy-start(f32[64,128]{1,0:T(8,128)} %get-tuple-element.192) | copy-start | bytes 98308
  176.4 10.6 %copy-start.28 = (f32[64,128]{1,0:T(8,128)S(1)}, f32[64,128]{1,0:T(8,128)}, u32[]{:S(2)}) copy-start(f32[64,128]{1,0:T(8,128)} %get-tuple-element.305) | copy-start | bytes 98308
  176.4 10.6 %copy-start.29 = (f32[64,128]{1,0:T(8,128)S(1)}, f32[64,128]{1,0:T(8,128)}, u32[]{:S(2)}) copy-start(f32[64,128]{1,0:T(8,128)} %get-tuple-element.306) | copy-start | bytes 98308
  176.4 10.6 %copy-start.30 = (f32[64,128]{1,0:T(8,128)S(1)}, f32[64,128]{1,0:T(8,128)}, u32[]{:S(2)}) copy-start(f32[64,128]{1,0:T(8,128)} %get-tuple-element.289) | copy-start | bytes 98308
  176.4 10.6 %copy-start.31 = (f32[64,128]{1,0:T(8,128)S(1)}, f32[64,128]{1,0:T(8,128)}, u32[]{:S(2)}) copy-start(f32[64,128]{1,0:T(8,128)} %get-tuple-element.290) | copy-start | bytes 98308
  176.4 10.6 %copy-start.32 = (f32[64,128]{1,0:T(8,128)S(1)}, f32[64,128]{1,0:T(8,128)}, u32[]{:S(2)}) copy-start(f32[64,128]{1,0:T(8,128)} %get-tuple-element.291) | copy-start | bytes 98308
  176.5 10.6 %copy-start.33 = (f32[64,128]{1,0:T(8,128)S(1)}, f32[64,128]{1,0:T(8,128)}, u32[]{:S(2)}) copy-start(f32[64,128]{1,0:T(8,128)} %get-tuple-element.292) | copy-start | bytes 98308
  176.5 10.6 %copy-start.34 = (f32[64,128]{1,0:T(8,128)S(1)}, f32[64,128]{1,0:T(8,128)}, u32[]{:S(2)}) copy-start(f32[64,128]{1,0:T(8,128)} %get-tuple-element.293) | copy-start | bytes 98308
  176.5 10.6 %copy-start.35 = (f32[64,128]{1,0:T(8,128)S(1)}, f32[64,128]{1,0:T(8,128)}, u32[]{:S(2)}) copy-start(f32[64,128]{1,0:T(8,128)} %get-tuple-element.294) | copy-start | bytes 98308
  176.5 10.6 %copy-start.36 = (f32[64,128]{1,0:T(8,128)S(1)}, f32[64,128]{1,0:T(8,128)}, u32[]{:S(2)}) copy-start(f32[64,128]{1,0:T(8,128)} %get-tuple-element.295) | copy-start | bytes 98308
  176.5 10.6 %copy-start.37 = (f32[64,128]{1,0:T(8,128)S(1)}, f32[64,128]{1,0:T(8,128)}, u32[]{:S(2)}) copy-start(f32[64,128]{1,0:T(8,128)} %get-tuple-element.296) | copy-start | bytes 98308
  176.5 10.6 %copy-start.38 = (f32[64,128]{1,0:T(8,128)S(1)}, f32[64,128]{1,0:T(8,128)}, u32[]{:S(2)}) copy-start(f32[64,128]{1,0:T(8,128)} %get-tuple-element.297) | copy-start | bytes 98308
  176.5 10.6 %copy-start.39 = (f32[64,128]{1,0:T(8,128)S(1)}, f32[64,128]{1,0:T(8,128)}, u32[]{:S(2)}) copy-start(f32[64,128]{1,0:T(8,128)} %get-tuple-element.298) | copy-start | bytes 98308
  176.5 10.6 %copy-start.40 = (f32[64,128]{1,0:T(8,128)S(1)}, f32[64,128]{1,0:T(8,128)}, u32[]{:S(2)}) copy-start(f32[64,128]{1,0:T(8,128)} %get-tuple-element.299) | copy-start | bytes 98308
  176.5 10.6 %copy-start.41 = (f32[64,128]{1,0:T(8,128)S(1)}, f32[64,128]{1,0:T(8,128)}, u32[]{:S(2)}) copy-start(f32[64,128]{1,0:T(8,128)} %get-tuple-element.300) | copy-start | bytes 98308
  191.0 23.2 %copy-start.8 = (f32[1,1,4,36,64,128]{5,4,3,2,1,0:T(8,128)}, f32[1,1,4,36,64,128]{5,4,3,2,1,0:T(8,128)S(1)}, u32[]{:S(2)}) copy-start(f32[1,1,4,36,64,128]{5,4,3,2,1,0:T(8,128)S(1)} %constant_dynamic-update-slice_fusion.2) | copy-start | bytes 14155780
  191.6 7.5 collective-permute-start.2
  199.1 7.5 collective-permute-start.3
  206.6 7.5 collective-permute-start.4
  214.1 13.3 %collective-permute-start.5 = (f32[1,1,5,64,128]{4,3,2,1,0:T(8,128)S(1)}, f32[1,1,5,64,128]{4,3,2,1,0:T(8,128)S(1)}, u32[]{:S(2)}, u32[]{:S(2)}) collective-permute-start(f32[1,1,5,64,128]{4,3,2,1,0:T(8,128)S(1)} %collective-permute-done.4), channel_id=1, source_target_pairs={{0,8},{8,16},{16,24},{24,32},{32,40},{40,48},{48,56},{56,64},{64,7... | collective-permute-start | bytes 491528 | tf_op jit(solution)/shard_map/ppermute | solution.py:321
  227.4 7.6 collective-permute-start.6
  235.0 7.7 collective-permute-start.7
  242.6 8.7 collective-permute-start.8
  251.4 8.9 %collective-permute-start.9 = (f32[1,1,5,64,128]{4,3,2,1,0:T(8,128)S(1)}, f32[1,1,5,64,128]{4,3,2,1,0:T(8,128)S(1)}, u32[]{:S(2)}, u32[]{:S(2)}) collective-permute-start(f32[1,1,5,64,128]{4,3,2,1,0:T(8,128)S(1)} %collective-permute-done.8), channel_id=1, source_target_pairs={{0,8},{8,16},{16,24},{24,32},{32,40},{40,48},{48,56},{56,64},{64,7... | collective-permute-start | bytes 491528 | tf_op jit(solution)/shard_map/ppermute | solution.py:321
  260.2 7.9 collective-permute-start.10
  268.2 7.5 collective-permute-start.11
  275.7 7.5 collective-permute-start.12
  283.2 7.5 collective-permute-start.13
  290.7 7.7 collective-permute-start.14
  298.3 7.7 collective-permute-start.15
  306.0 8.7 collective-permute-start.16
  316.7 38.0 %collective-permute-start.18 = (f32[1,2,128]{2,1,0:T(2,128)S(1)}, f32[1,2,128]{2,1,0:T(2,128)S(1)}, u32[]{:S(2)}, u32[]{:S(2)}) collective-permute-start(f32[1,2,128]{2,1,0:T(2,128)S(1)} %bitcast.729), channel_id=1, source_target_pairs={{0,1},{1,2},{2,3},{3,4},{4,5},{5,6},{6,7},{8,9},{9,10},{10,11},{11... | collective-permute-start | bytes 3080 | tf_op jit(solution)/shard_map/ppermute | solution.py:18
  336.3 36.3 %collective-permute-start.17 = (f32[1,2,128]{2,1,0:T(2,128)S(1)}, f32[1,2,128]{2,1,0:T(2,128)S(1)}, u32[]{:S(2)}, u32[]{:S(2)}) collective-permute-start(f32[1,2,128]{2,1,0:T(2,128)S(1)} %bitcast.728), channel_id=1, source_target_pairs={{1,0},{2,1},{3,2},{4,3},{5,4},{6,5},{7,6},{9,8},{10,9},{11,10},{12... | collective-permute-start | bytes 3080 | tf_op jit(solution)/shard_map/ppermute | solution.py:18
  555.1 10.1 %collective-permute-start.20 = (f32[1,2,128]{2,1,0:T(2,128)S(1)}, f32[1,2,128]{2,1,0:T(2,128)S(1)}, u32[]{:S(2)}, u32[]{:S(2)}) collective-permute-start(f32[1,2,128]{2,1,0:T(2,128)S(1)} %bitcast.731), channel_id=1, source_target_pairs={{0,1},{1,2},{2,3},{3,4},{4,5},{5,6},{6,7},{8,9},{9,10},{10,11},{11... | collective-permute-start | bytes 3080 | tf_op jit(solution)/shard_map/ppermute | solution.py:18
  562.4 20.4 %collective-permute-start.19 = (f32[1,2,128]{2,1,0:T(2,128)S(1)}, f32[1,2,128]{2,1,0:T(2,128)S(1)}, u32[]{:S(2)}, u32[]{:S(2)}) collective-permute-start(f32[1,2,128]{2,1,0:T(2,128)S(1)} %bitcast.727), channel_id=1, source_target_pairs={{1,0},{2,1},{3,2},{4,3},{5,4},{6,5},{7,6},{9,8},{10,9},{11,10},{12... | collective-permute-start | bytes 3080 | tf_op jit(solution)/shard_map/ppermute | solution.py:18
  759.4 10.4 %collective-permute-start.21 = (f32[1,2,128]{2,1,0:T(2,128)S(1)}, f32[1,2,128]{2,1,0:T(2,128)S(1)}, u32[]{:S(2)}, u32[]{:S(2)}) collective-permute-start(f32[1,2,128]{2,1,0:T(2,128)S(1)} %bitcast.732), channel_id=1, source_target_pairs={{1,0},{2,1},{3,2},{4,3},{5,4},{6,5},{7,6},{9,8},{10,9},{11,10},{12... | collective-permute-start | bytes 3080 | tf_op jit(solution)/shard_map/ppermute | solution.py:18
  767.8 19.0 %collective-permute-start.22 = (f32[1,2,128]{2,1,0:T(2,128)S(1)}, f32[1,2,128]{2,1,0:T(2,128)S(1)}, u32[]{:S(2)}, u32[]{:S(2)}) collective-permute-start(f32[1,2,128]{2,1,0:T(2,128)S(1)} %bitcast.730), channel_id=1, source_target_pairs={{0,1},{1,2},{2,3},{3,4},{4,5},{5,6},{6,7},{8,9},{9,10},{10,11},{11... | collective-permute-start | bytes 3080 | tf_op jit(solution)/shard_map/ppermute | solution.py:18
  (14 other events, 93.9 us)
Sparse Core Ops, SparseCore 0:
  10.1 45.1 all-gather.7
  58.1 42.7 all-gather.3
  103.1 43.9 all-gather.5
